TPU v7x, 128 devices: a whole 4x4x4 slice. The times are simulated.
128 devices in a mesh: req: 32 (over z, y, core), head: 4 (over x).
Axes of the slice: x: 4, y: 4, z: 4, core: 2. Of those that a mesh axis runs over, the one named last changes fastest.
Arguments:
- hidden_in: bfloat16 [512, 2048], P(None, 'req'), may hold values from -6 to 6
- lengths: int32 [512], P('req'), may hold values from 16 to 3072, as said below
- w_qkv: bfloat16 [3, 2048, 2048], P(None, 'req', 'head'), may hold values from -4 to 4, as said below
- qk_gain: float32 [2, 2048], P(None, 'head'), may hold values from 0.25 to 1.75
- cache_keys: bfloat16 [131072, 2048], P('req', 'head'), may hold values from -240 to 240
- cache_values: bfloat16 [131072, 2048], P('req', 'head'), may hold values from -6 to 6
- w_out: bfloat16 [2048, 2048], P('req', 'head'), may hold values from -3 to 3, as said below
- norm_gain: float32 [2, 2048], P(None, 'req'), may hold values from 0.25 to 1.75
- w_gate_up: bfloat16 [2, 2048, 8192], P(None, 'req', 'head'), may hold values from -0.125 to 0.125
- w_down: bfloat16 [2048, 8192], P('req', 'head'), may hold values from -3 to 3, as said below
Outputs:
- hidden_out: bfloat16 [512, 2048], P(None, 'req')
- new_keys: bfloat16 [512, 2048], P('req', 'head')
- new_values: bfloat16 [512, 2048], P('req', 'head')
Inputs may be any that keep to these rules, and one draw needn't show every extreme that they name: `lengths`: in each aligned group of requests 8 * 16 * k to 8 * 16 * k + 8 * 16 - 1 exactly one request, at a place drawn from the seed, has length 3072; every other length lies between 16 and 64. `w_qkv`: entries have magnitude at most 26 / sqrt(2048). `w_out`: entries have magnitude at most 23 / sqrt(2048). `w_down`: entries have magnitude at most 23 / sqrt(8192).
All inputs are finite; a program needn't handle non-finite values.
Results may differ from a plain program's by a relative error of at most 0.015.
Values may be sent and summed in bfloat16 or wider, within the bound.
No kernel may reach another device: no remote copies, remote signals or barrier semaphores. Data moves between devices by JAX's collectives and lax.ppermute only.
A program may use at most 128 MiB of HBM per device.

v0:
```python
import jax
import jax.numpy as jnp
from jax import lax
from jax.sharding import PartitionSpec as P

HEAD_DIM = 128
EPS = 1e-06
THETA = 500000.0


def rotate(values, positions):
    half = values.shape[-1] // 2
    freqs = jnp.power(THETA, -(jnp.arange(half, dtype=jnp.float32) * 2.0 / values.shape[-1]))
    angles = positions.astype(jnp.float32)[:, None] * freqs[None, :]
    cosine = jnp.cos(angles)[:, None, :]
    sine = jnp.sin(angles)[:, None, :]
    first = values[..., :half]
    second = values[..., half:]
    return jnp.concatenate(
        [first * cosine - second * sine, second * cosine + first * sine], axis=-1
    )


def contract_last(left, right):
    return lax.dot_general(
        left, right, (((1,), (1,)), ((), ())), preferred_element_type=jnp.float32
    )


def body(
    hidden_in,
    lengths,
    w_qkv,
    qk_gain,
    cache_keys,
    cache_values,
    w_out,
    norm_gain,
    w_gate_up,
    w_down,
):
    rows_here = lengths.shape[0]
    width_here = w_qkv.shape[2]
    heads_here = width_here // HEAD_DIM
    units_here = w_gate_up.shape[2]
    full_width = width_here * lax.axis_size("head")
    model_width = hidden_in.shape[1] * lax.axis_size("req")
    selected = hidden_in
    product = jnp.einsum("bd,gdf->bgf", selected, w_qkv, preferred_element_type=jnp.float32)
    projected = lax.psum_scatter(
        product.reshape(rows_here * lax.axis_size("req"), 3 * width_here),
        "req",
        scatter_dimension=0,
        tiled=True,
    )
    query = projected[:, :width_here]
    key_new = projected[:, width_here : 2 * width_here]
    value_new = projected[:, 2 * width_here :].astype(jnp.bfloat16)
    query_squares, key_squares = lax.psum(
        (jnp.sum(query * query, axis=1), jnp.sum(key_new * key_new, axis=1)), "head"
    )
    query = query * lax.rsqrt(query_squares[:, None] / full_width + EPS) * qk_gain[0]
    key_new = key_new * lax.rsqrt(key_squares[:, None] / full_width + EPS) * qk_gain[1]
    query_rot = rotate(query.reshape(rows_here, heads_here, HEAD_DIM), lengths).astype(jnp.bfloat16)
    key_rot = rotate(key_new.reshape(rows_here, heads_here, HEAD_DIM), lengths).astype(jnp.bfloat16)
    value_heads = value_new.reshape(rows_here, heads_here, HEAD_DIM)
    scale = HEAD_DIM ** (-0.5)
    starts = jnp.cumsum(lengths) - lengths
    ends = starts + lengths
    own_score = jnp.sum(query_rot.astype(jnp.float32) * key_rot.astype(jnp.float32), axis=2) * scale
    pool_rows = cache_keys.shape[0]
    block = 512

    def attend_block(index, carry):
        running_max, running_total, running_sum = carry
        offset = index * block
        block_keys = lax.dynamic_slice_in_dim(cache_keys, offset, block, 0).reshape(
            block, heads_here, HEAD_DIM
        )
        block_values = lax.dynamic_slice_in_dim(cache_values, offset, block, 0).reshape(
            block, heads_here, HEAD_DIM
        )
        scores = (
            jnp.einsum("rhd,phd->rhp", query_rot, block_keys, preferred_element_type=jnp.float32)
            * scale
        )
        positions = offset + jnp.arange(block, dtype=jnp.int32)
        inside = (positions[None, :] >= starts[:, None]) & (positions[None, :] < ends[:, None])
        scores = jnp.where(inside[:, None, :], scores, -jnp.inf)
        new_max = jnp.maximum(running_max, jnp.max(scores, axis=2))
        weights = jnp.exp(scores - new_max[:, :, None]).astype(jnp.bfloat16)
        factor = jnp.exp(running_max - new_max)
        running_total = running_total * factor + jnp.sum(weights.astype(jnp.float32), axis=2)
        running_sum = running_sum * factor[:, :, None] + jnp.einsum(
            "rhp,phd->rhd", weights, block_values, preferred_element_type=jnp.float32
        )
        return (new_max, running_total, running_sum)

    steps_count = pool_rows // block
    initial = (own_score, jnp.ones_like(own_score), value_heads.astype(jnp.float32))
    final_max, final_total, final_sum = lax.fori_loop(0, steps_count, attend_block, initial)
    attended = (
        (final_sum / final_total[:, :, None]).astype(jnp.bfloat16).reshape(rows_here, width_here)
    )
    attn_part = contract_last(lax.all_gather(attended, "req", axis=0, tiled=True), w_out)
    attn_full = lax.psum(attn_part, "head")
    attn_power = lax.psum(jnp.sum(attn_full * attn_full, axis=1), "req")
    attn_normed = attn_full * lax.rsqrt(attn_power[:, None] / model_width + EPS) * norm_gain[0]
    hidden_mid = (hidden_in.astype(jnp.float32) + attn_normed).astype(jnp.bfloat16)
    selected = hidden_mid
    product = jnp.einsum("bd,gdf->bgf", selected, w_gate_up, preferred_element_type=jnp.float32)
    combined = lax.psum_scatter(
        product.reshape(rows_here * lax.axis_size("req"), 2 * units_here),
        "req",
        scatter_dimension=0,
        tiled=True,
    )
    gated = combined[:, :units_here]
    lifted = combined[:, units_here:]
    activated = (jax.nn.silu(gated) * lifted).astype(jnp.bfloat16)
    down_part = contract_last(lax.all_gather(activated, "req", axis=0, tiled=True), w_down)
    ffn_full = lax.psum(down_part, "head")
    ffn_power = lax.psum(jnp.sum(ffn_full * ffn_full, axis=1), "req")
    ffn_normed = ffn_full * lax.rsqrt(ffn_power[:, None] / model_width + EPS) * norm_gain[1]
    hidden_out = (hidden_mid.astype(jnp.float32) + ffn_normed).astype(jnp.bfloat16)
    return (hidden_out, key_rot.reshape(rows_here, width_here), value_new)


def solution(mesh):
    return jax.shard_map(
        body,
        mesh=mesh,
        in_specs=(
            P(None, "req"),
            P("req"),
            P(None, "req", "head"),
            P(None, "head"),
            P("req", "head"),
            P("req", "head"),
            P("req", "head"),
            P(None, "req"),
            P(None, "req", "head"),
            P("req", "head"),
        ),
        out_specs=(P(None, "req"), P("req", "head"), P("req", "head")),
        check_vma=False,
    )
```

profile of v0, /device:TPU:0, one launch (start us, length us, event | category | flops | bytes accessed | tf_op | source)
XLA Modules:
  0.0 528.0 jit_solution(12049688516893260932)
XLA Ops:
  7.2 3.3 fusion.7
  10.6 3.6 copy.52
  14.6 82.7 %reduce-scatter.5.cloned.1.call-done = f32[16,1536]{1,0:T(8,128)} async-done(((f32[512,1536]{1,0:T(8,128)}), f32[16,1536]{1,0:T(8,128)}) %reduce-scatter.5.cloned.1.call-update) | async-done | bytes 98320 | tf_op jit(solution)/shard_map/reduce_scatter | solution.py:50
  97.3 0.9 multiply_reduce_fusion.4
  98.2 10.5 %all-reduce = (f32[16]{0:T(128)S(1)}, f32[16]{0:T(128)S(1)}) all-reduce(f32[16]{0:T(128)S(1)} %get-tuple-element.227, f32[16]{0:T(128)S(1)} %get-tuple-element.226), channel_id=1, replica_groups=mesh['req'=32,'head'=4] {'head'}, use_global_device_ids=true, to_apply=%region_4.0 | all-reduce | flops 32 | bytes 256 | tf_op jit(solution)/shard_map/psum | solution.py:59
  108.7 0.9 multiply_multiply_fusion
  109.5 1.4 convert_bitcast_fusion
  111.3 20.6 %while.18 = (s32[]{:T(128)}, f32[16,4]{0,1:T(4,128)S(1)}, f32[16,4]{0,1:T(4,128)S(1)}, f32[16,4,128]{2,0,1:T(8,128)S(1)}, s32[16]{0:T(128)S(1)}, /*index=5*/s32[...) while((s32[]{:T(128)}, f32[16,4]{0,1:T(4,128)S(1)}, ...), condition=%wide.region_10.11_spmd.clone, body=%wide.region_7.10_spmd.clone.sunk | while | flops 17113800 | bytes 5742917 | solution.py:101
  111.4 1.3 constant_dynamic-slice_fusion.3
  113.0 0.3 fusion.37
  113.7 0.3 fusion.39
  114.0 1.3 constant_dynamic-slice_fusion.3
  115.5 0.3 fusion.37
  116.2 0.3 fusion.39
  116.6 1.3 constant_dynamic-slice_fusion.3
  118.1 0.3 fusion.37
  118.8 0.3 fusion.39
  119.2 1.3 constant_dynamic-slice_fusion.3
  120.7 0.3 fusion.37
  121.4 0.3 fusion.39
  121.8 1.3 constant_dynamic-slice_fusion.3
  123.3 0.3 fusion.37
  124.0 0.3 fusion.39
  124.3 1.3 constant_dynamic-slice_fusion.3
  125.8 0.3 fusion.37
  126.5 0.3 fusion.39
  126.9 1.3 constant_dynamic-slice_fusion.3
  128.4 0.3 fusion.37
  129.1 0.3 fusion.39
  129.5 1.3 constant_dynamic-slice_fusion.3
  131.7 0.3 fusion.39
  132.1 24.1 %all_gather.6 = bf16[512,512]{1,0:T(8,128)(2,1)S(1)} all-gather(bf16[16,512]{1,0:T(8,128)(2,1)S(1)} %copy_bitcast_fusion.2), channel_id=1, replica_groups=mesh['req'=32,'head'=4] {'req'}, dimensions={0}, use_global_device_ids=true | all-gather | bytes 540672 | tf_op jit(solution)/shard_map/all_gather | solution.py:105
  156.2 0.9 fusion.15
  157.3 37.5 %all-reduce.4.cloned.1.call-done = f32[512,64]{0,1:T(8,128)} async-done(((f32[512,64]{0,1:T(8,128)}), f32[512,64]{0,1:T(8,128)}) %all-reduce.4.cloned.1.call-update) | async-done | bytes 131088 | tf_op jit(solution)/shard_map/psum | solution.py:106
  194.8 0.9 multiply_reduce_fusion.1
  195.7 65.2 %psum.45 = f32[512]{0:T(512)S(1)} all-reduce(f32[512]{0:T(512)S(1)} %multiply_reduce_fusion.1), channel_id=1, replica_groups=mesh['req'=32,'head'=4] {'req'}, use_global_device_ids=true, to_apply=%region_13.14 | all-reduce | flops 512 | bytes 4096 | tf_op jit(solution)/shard_map/psum | solution.py:107
  260.9 1.0 add_convert_fusion.1
  261.9 4.5 fusion.5
  266.4 8.9 %copy.69 = f32[512,4096]{1,0:T(8,128)} copy(f32[512,4096]{0,1:T(8,128)} %bitcast.64) | data formatting | bytes 16777216
  275.4 88.6 %reduce-scatter.7.cloned.1.call-done = f32[16,4096]{1,0:T(8,128)} async-done(((f32[512,4096]{1,0:T(8,128)}), f32[16,4096]{1,0:T(8,128)}) %reduce-scatter.7.cloned.1.call-update) | async-done | bytes 262160 | tf_op jit(solution)/shard_map/reduce_scatter | solution.py:112
  364.0 1.6 fusion.4
  365.7 44.5 %all-gather.2.cloned.1.call-done = bf16[512,2048]{1,0:T(8,128)(2,1)} async-done(((bf16[16,2048]{1,0:T(8,128)(2,1)}), bf16[512,2048]{1,0:T(8,128)(2,1)}) %all-gather.2.cloned.1.call-update) | async-done | bytes 2097168 | tf_op jit(solution)/shard_map/all_gather | solution.py:121
  410.2 3.0 fusion.16
  413.3 0.6 copy_bitcast_fusion.1
  413.9 39.9 %all-reduce.6.cloned.1.call-done = f32[512,64]{0,1:T(8,128)} async-done(((f32[512,64]{0,1:T(8,128)}), f32[512,64]{0,1:T(8,128)}) %all-reduce.6.cloned.1.call-update) | async-done | bytes 131088 | tf_op jit(solution)/shard_map/psum | solution.py:122
  453.7 0.9 multiply_reduce_fusion
  454.7 65.2 %psum.47 = f32[512]{0:T(512)S(1)} all-reduce(f32[512]{0:T(512)S(1)} %multiply_reduce_fusion), channel_id=1, replica_groups=mesh['req'=32,'head'=4] {'req'}, use_global_device_ids=true, to_apply=%region_17.18 | all-reduce | flops 512 | bytes 4096 | tf_op jit(solution)/shard_map/psum | solution.py:123
  519.8 1.6 add_convert_fusion
  (111 shorter events, 7.3 us)
Async XLA Ops:
  7.2 254.7 %copy-start = (bf16[2,64,2048]{2,1,0:T(8,128)(2,1)S(1)}, bf16[2,64,2048]{2,1,0:T(8,128)(2,1)}, u32[]{:S(2)}) copy-start(bf16[2,64,2048]{2,1,0:T(8,128)(2,1)} %param.20) | copy-start | bytes 1572868
  7.2 90.1 %reduce-scatter.5.cloned.1.call-start = ((), (), s32[]{:S(2)}) async-start(), calls=%async_computation.2 | async-start | bytes 3244032 | tf_op jit(solution)/shard_map/reduce_scatter | solution.py:50
  10.6 3.7 copy-start.5
  10.6 3.9 copy-start.4
  14.2 180.6 %all-reduce.4.cloned.1.call-start = ((), (), s32[]{:S(2)}) async-start(), calls=%async_computation.3 | async-start | bytes 262144 | tf_op jit(solution)/shard_map/psum | solution.py:106
  111.3 44.9 %copy-start.3 = (bf16[64,512]{1,0:T(8,128)(2,1)S(1)}, bf16[64,512]{1,0:T(8,128)(2,1)}, u32[]{:S(2)}) copy-start(bf16[64,512]{1,0:T(8,128)(2,1)} %param.18) | copy-start | bytes 196612
  111.3 45.9 %copy-start.6 = (f32[2,64]{1,0:T(2,128)S(1)}, f32[2,64]{1,0:T(2,128)}, u32[]{:S(2)}) copy-start(f32[2,64]{1,0:T(2,128)} %param.19) | copy-start | bytes 1540
  111.3 149.6 %copy-start.2 = (bf16[512,64]{0,1:T(8,128)(2,1)S(1)}, bf16[512,64]{0,1:T(8,128)(2,1)}, u32[]{:S(2)}) copy-start(bf16[512,64]{0,1:T(8,128)(2,1)} %param.12) | copy-start | bytes 196612
  157.2 206.8 %reduce-scatter.7.cloned.1.call-start = ((), (), s32[]{:S(2)}) async-start(), calls=%async_computation.6 | async-start | bytes 8650752 | tf_op jit(solution)/shard_map/reduce_scatter | solution.py:112
  275.3 134.9 %copy-start.1 = (bf16[64,2048]{1,0:T(8,128)(2,1)S(1)}, bf16[64,2048]{1,0:T(8,128)(2,1)}, u32[]{:S(2)}) copy-start(bf16[64,2048]{1,0:T(8,128)(2,1)} %param.21) | copy-start | bytes 786436
  275.4 134.9 %all-gather.2.cloned.1.call-start = ((), (), s32[]{:S(2)}) async-start(), calls=%async_computation.4 | async-start | bytes 2162688 | tf_op jit(solution)/shard_map/all_gather | solution.py:121
  365.7 88.1 %all-reduce.6.cloned.1.call-start = ((), (), s32[]{:S(2)}) async-start(), calls=%async_computation.5 | async-start | bytes 262144 | tf_op jit(solution)/shard_map/psum | solution.py:122
Sparse Core Ops, SparseCore 0:
  14.3 82.9 reduce-scatter.4
  157.3 37.4 all-reduce.3
  275.5 88.4 reduce-scatter.6
  367.0 43.2 all-gather.1
  413.4 40.3 all-reduce.5
where the time goes:
time: 529 us; the launch traced here: 528 us
  waiting for transfers between devices  293 us (55%)
  blocking collectives  165 us (31%)
  local copies, waits for them, and re-layouts  27.1 us (5%)
  matrix products  16.1 us (3%)
  between operations  13.9 us (3%)
  other arithmetic  12.2 us (2%)
    reduce_scatter x1, waiting for transfers between devices, body(): lax.psum_scatter(product.reshape(rows_here * lax.axis_size('req'), 2 * un...  88.6 us
    reduce_scatter x1, waiting for transfers between devices, body(): lax.psum_scatter(product.reshape(rows_here * lax.axis_size('req'), 3 * wi...  82.7 us
    psum x1, blocking collectives, body(): attn_power = lax.psum(jnp.sum(attn_full * attn_full, axis=1), 'req')  65.2 us
    psum x1, blocking collectives, body(): ffn_power = lax.psum(jnp.sum(ffn_full * ffn_full, axis=1), 'req')  65.2 us
    all_gather x1, waiting for transfers between devices, body(): lax.all_gather(activated, 'req', axis=0, tiled=True)  44.5 us
    psum x1, waiting for transfers between devices, body(): ffn_full = lax.psum(down_part, 'head')  39.9 us
    psum x1, waiting for transfers between devices, body(): attn_full = lax.psum(attn_part, 'head')  37.5 us
    all_gather x1, blocking collectives, body(): lax.all_gather(attended, 'req', axis=0, tiled=True)  24.1 us
  transfers between devices with their start and end apart: 5, of which 5 were waited for; matrix products, arithmetic and copies ran while one was open for 0% of the time, Pallas kernels for 0%

commit v1 on v0

--- a/solution.py
+++ b/solution.py
@@ -104,7 +104,7 @@
     )
     attn_part = contract_last(lax.all_gather(attended, "req", axis=0, tiled=True), w_out)
     attn_full = lax.psum(attn_part, "head")
-    attn_power = lax.psum(jnp.sum(attn_full * attn_full, axis=1), "req")
+    attn_power = jnp.sum(lax.all_gather(jnp.sum(attn_full * attn_full, axis=1), "req"), axis=0)
     attn_normed = attn_full * lax.rsqrt(attn_power[:, None] / model_width + EPS) * norm_gain[0]
     hidden_mid = (hidden_in.astype(jnp.float32) + attn_normed).astype(jnp.bfloat16)
     selected = hidden_mid

time: 529 us -> 491 us (0.928)
  blocking collectives: 165 us -> 124 us
    psum x1 -> x0, blocking collectives: 65.2 us -> none  [body(): attn_power = lax.psum(jnp.sum(attn_full * attn_full, axis=1), 'req')]
    all_gather x0 -> x1, blocking collectives: none -> 24.4 us  [body(): lax.all_gather(jnp.sum(attn_full * attn_full, axis=1), 'req')]
where the time goes in v1:
time: 491 us; the launch traced here: 490 us
  waiting for transfers between devices  296 us (60%)
  blocking collectives  124 us (25%)
  local copies, waits for them, and re-layouts  27.1 us (6%)
  matrix products  16.1 us (3%)
  between operations  13.9 us (3%)
  other arithmetic  12.2 us (2%)
    reduce_scatter x1, waiting for transfers between devices, body(): lax.psum_scatter(product.reshape(rows_here * lax.axis_size('req'), 2 * un...  91.4 us
    reduce_scatter x1, waiting for transfers between devices, body(): lax.psum_scatter(product.reshape(rows_here * lax.axis_size('req'), 3 * wi...  82.7 us
    psum x1, blocking collectives, body(): ffn_power = lax.psum(jnp.sum(ffn_full * ffn_full, axis=1), 'req')  65.2 us
    all_gather x1, waiting for transfers between devices, body(): lax.all_gather(activated, 'req', axis=0, tiled=True)  44.5 us
    psum x1, waiting for transfers between devices, body(): ffn_full = lax.psum(down_part, 'head')  39.9 us
    psum x1, waiting for transfers between devices, body(): attn_full = lax.psum(attn_part, 'head')  37.5 us
    all_gather x1, blocking collectives, body(): lax.all_gather(jnp.sum(attn_full * attn_full, axis=1), 'req')  24.4 us
    all_gather x1, blocking collectives, body(): lax.all_gather(attended, 'req', axis=0, tiled=True)  24.1 us
  transfers between devices with their start and end apart: 5, of which 5 were waited for; matrix products, arithmetic and copies ran while one was open for 0% of the time, Pallas kernels for 0%

profile of v1, /device:TPU:0, one launch (start us, length us, event | category | flops | bytes accessed | tf_op | source)
XLA Modules:
  0.0 490.1 jit_solution(1127628851556736123)
XLA Ops:
  7.2 3.3 fusion.7
  10.6 3.6 copy.52
  14.6 82.7 %reduce-scatter.5.cloned.1.call-done = f32[16,1536]{1,0:T(8,128)} async-done(((f32[512,1536]{1,0:T(8,128)}), f32[16,1536]{1,0:T(8,128)}) %reduce-scatter.5.cloned.1.call-update) | async-done | bytes 98320 | tf_op jit(solution)/shard_map/reduce_scatter | solution.py:50
  97.3 0.9 multiply_reduce_fusion.4
  98.2 10.5 %all-reduce = (f32[16]{0:T(128)S(1)}, f32[16]{0:T(128)S(1)}) all-reduce(f32[16]{0:T(128)S(1)} %get-tuple-element.227, f32[16]{0:T(128)S(1)} %get-tuple-element.226), channel_id=1, replica_groups=mesh['req'=32,'head'=4] {'head'}, use_global_device_ids=true, to_apply=%region_4.0 | all-reduce | flops 32 | bytes 256 | tf_op jit(solution)/shard_map/psum | solution.py:59
  108.7 0.9 multiply_multiply_fusion
  109.5 1.4 convert_bitcast_fusion
  111.3 20.6 %while.18 = (s32[]{:T(128)}, f32[16,4]{0,1:T(4,128)S(1)}, f32[16,4]{0,1:T(4,128)S(1)}, f32[16,4,128]{2,0,1:T(8,128)S(1)}, s32[16]{0:T(128)S(1)}, /*index=5*/s32[...) while((s32[]{:T(128)}, f32[16,4]{0,1:T(4,128)S(1)}, ...), condition=%wide.region_10.11_spmd.clone, body=%wide.region_7.10_spmd.clone.sunk | while | flops 17113800 | bytes 5742917 | solution.py:101
  111.4 1.3 constant_dynamic-slice_fusion.3
  113.0 0.3 fusion.37
  113.7 0.3 fusion.39
  114.0 1.3 constant_dynamic-slice_fusion.3
  115.5 0.3 fusion.37
  116.2 0.3 fusion.39
  116.6 1.3 constant_dynamic-slice_fusion.3
  118.1 0.3 fusion.37
  118.8 0.3 fusion.39
  119.2 1.3 constant_dynamic-slice_fusion.3
  120.7 0.3 fusion.37
  121.4 0.3 fusion.39
  121.8 1.3 constant_dynamic-slice_fusion.3
  123.3 0.3 fusion.37
  124.0 0.3 fusion.39
  124.3 1.3 constant_dynamic-slice_fusion.3
  125.8 0.3 fusion.37
  126.5 0.3 fusion.39
  126.9 1.3 constant_dynamic-slice_fusion.3
  128.4 0.3 fusion.37
  129.1 0.3 fusion.39
  129.5 1.3 constant_dynamic-slice_fusion.3
  131.7 0.3 fusion.39
  132.1 24.1 %all_gather.12 = bf16[512,512]{1,0:T(8,128)(2,1)S(1)} all-gather(bf16[16,512]{1,0:T(8,128)(2,1)S(1)} %copy_bitcast_fusion.2), channel_id=1, replica_groups=mesh['req'=32,'head'=4] {'req'}, dimensions={0}, use_global_device_ids=true | all-gather | bytes 540672 | tf_op jit(solution)/shard_map/all_gather | solution.py:105
  156.2 0.9 fusion.15
  157.3 37.5 %all-reduce.4.cloned.1.call-done = f32[512,64]{0,1:T(8,128)} async-done(((f32[512,64]{0,1:T(8,128)}), f32[512,64]{0,1:T(8,128)}) %all-reduce.4.cloned.1.call-update) | async-done | bytes 131088 | tf_op jit(solution)/shard_map/psum | solution.py:106
  194.8 0.9 multiply_reduce_fusion.1
  195.7 24.4 %all-gather.1 = f32[32,1,512]{2,1,0:T(1,128)S(1)} all-gather(f32[1,1,512]{2,1,0:T(1,128)S(1)} %bitcast.68), channel_id=2, replica_groups=mesh['req'=32,'head'=4] {'req'}, dimensions={0}, use_global_device_ids=true | all-gather | bytes 67584 | tf_op jit(solution)/shard_map/all_gather | solution.py:107
  220.2 1.0 add_convert_fusion.1
  221.2 4.5 fusion.5
  225.7 8.9 %copy.69 = f32[512,4096]{1,0:T(8,128)} copy(f32[512,4096]{0,1:T(8,128)} %bitcast.65) | data formatting | bytes 16777216
  234.7 91.4 %reduce-scatter.7.cloned.1.call-done = f32[16,4096]{1,0:T(8,128)} async-done(((f32[512,4096]{1,0:T(8,128)}), f32[16,4096]{1,0:T(8,128)}) %reduce-scatter.7.cloned.1.call-update) | async-done | bytes 262160 | tf_op jit(solution)/shard_map/reduce_scatter | solution.py:112
  326.1 1.6 fusion.4
  327.8 44.5 %all-gather.4.cloned.1.call-done = bf16[512,2048]{1,0:T(8,128)(2,1)} async-done(((bf16[16,2048]{1,0:T(8,128)(2,1)}), bf16[512,2048]{1,0:T(8,128)(2,1)}) %all-gather.4.cloned.1.call-update) | async-done | bytes 2097168 | tf_op jit(solution)/shard_map/all_gather | solution.py:121
  372.3 3.0 fusion.16
  375.4 0.6 copy_bitcast_fusion.1
  376.0 39.9 %all-reduce.6.cloned.1.call-done = f32[512,64]{0,1:T(8,128)} async-done(((f32[512,64]{0,1:T(8,128)}), f32[512,64]{0,1:T(8,128)}) %all-reduce.6.cloned.1.call-update) | async-done | bytes 131088 | tf_op jit(solution)/shard_map/psum | solution.py:122
  415.8 0.9 multiply_reduce_fusion
  416.8 65.2 %psum.39 = f32[512]{0:T(512)S(1)} all-reduce(f32[512]{0:T(512)S(1)} %multiply_reduce_fusion), channel_id=1, replica_groups=mesh['req'=32,'head'=4] {'req'}, use_global_device_ids=true, to_apply=%region_17.18 | all-reduce | flops 512 | bytes 4096 | tf_op jit(solution)/shard_map/psum | solution.py:123
  481.9 1.6 add_convert_fusion
  (112 shorter events, 7.3 us)
Async XLA Ops:
  7.2 214.0 %copy-start = (bf16[2,64,2048]{2,1,0:T(8,128)(2,1)S(1)}, bf16[2,64,2048]{2,1,0:T(8,128)(2,1)}, u32[]{:S(2)}) copy-start(bf16[2,64,2048]{2,1,0:T(8,128)(2,1)} %param.20) | copy-start | bytes 1572868
  7.2 90.1 %reduce-scatter.5.cloned.1.call-start = ((), (), s32[]{:S(2)}) async-start(), calls=%async_computation.2 | async-start | bytes 3244032 | tf_op jit(solution)/shard_map/reduce_scatter | solution.py:50
  10.6 3.7 copy-start.5
  10.6 3.9 copy-start.4
  14.2 180.6 %all-reduce.4.cloned.1.call-start = ((), (), s32[]{:S(2)}) async-start(), calls=%async_computation.3 | async-start | bytes 262144 | tf_op jit(solution)/shard_map/psum | solution.py:106
  111.3 44.9 %copy-start.3 = (bf16[64,512]{1,0:T(8,128)(2,1)S(1)}, bf16[64,512]{1,0:T(8,128)(2,1)}, u32[]{:S(2)}) copy-start(bf16[64,512]{1,0:T(8,128)(2,1)} %param.18) | copy-start | bytes 196612
  111.3 45.9 %copy-start.6 = (f32[2,64]{1,0:T(2,128)S(1)}, f32[2,64]{1,0:T(2,128)}, u32[]{:S(2)}) copy-start(f32[2,64]{1,0:T(2,128)} %param.19) | copy-start | bytes 1540
  111.3 108.9 %copy-start.2 = (bf16[512,64]{0,1:T(8,128)(2,1)S(1)}, bf16[512,64]{0,1:T(8,128)(2,1)}, u32[]{:S(2)}) copy-start(bf16[512,64]{0,1:T(8,128)(2,1)} %param.12) | copy-start | bytes 196612
  157.2 168.9 %reduce-scatter.7.cloned.1.call-start = ((), (), s32[]{:S(2)}) async-start(), calls=%async_computation.6 | async-start | bytes 8650752 | tf_op jit(solution)/shard_map/reduce_scatter | solution.py:112
  234.6 137.7 %copy-start.1 = (bf16[64,2048]{1,0:T(8,128)(2,1)S(1)}, bf16[64,2048]{1,0:T(8,128)(2,1)}, u32[]{:S(2)}) copy-start(bf16[64,2048]{1,0:T(8,128)(2,1)} %param.21) | copy-start | bytes 786436
  234.7 137.7 %all-gather.4.cloned.1.call-start = ((), (), s32[]{:S(2)}) async-start(), calls=%async_computation.4 | async-start | bytes 2162688 | tf_op jit(solution)/shard_map/all_gather | solution.py:121
  327.8 88.0 %all-reduce.6.cloned.1.call-start = ((), (), s32[]{:S(2)}) async-start(), calls=%async_computation.5 | async-start | bytes 262144 | tf_op jit(solution)/shard_map/psum | solution.py:122
Sparse Core Ops, SparseCore 0:
  14.3 82.9 reduce-scatter.4
  157.3 37.4 all-reduce.3
  234.8 91.2 reduce-scatter.6
  329.1 43.2 all-gather.3
  375.5 40.3 all-reduce.5
